TPU v7x, 128 devices: a whole 4x4x4 slice. The times are simulated.
128 devices in a mesh: freq: 16 (over x, z_lo, core), src: 8 (over y, z_hi).
Axes of the slice: x: 4, y: 4, z: 4 (z_hi: 2, z_lo: 2; z = z_hi * 2 + z_lo), core: 2. Of those that a mesh axis runs over, the one named last changes fastest.
Arguments:
- focusing: bfloat16 [64, 1024, 2048], P('src', 'freq'), may hold values from -6 to 6
- direct: bfloat16 [64, 1024, 2048], P('src', 'freq'), may hold values from -6 to 6
- kernel: bfloat16 [2, 192, 2048, 1024], P(None, 'freq', 'src'), may hold values from -0.125 to 0.125
- onset_up: int32 [64, 2048], P('freq', 'src'), may hold values from 256 to 2048
- onset_back: int32 [64, 1024], P('src', 'freq'), may hold values from 256 to 2048
Outputs:
- upgoing: bfloat16 [64, 2048, 2048], P('freq', 'src')
- updated: bfloat16 [64, 1024, 2048], P('src', 'freq')
All inputs are finite; a program needn't handle non-finite values.
Results may differ from a plain program's by a relative error of at most 0.008.
Values may be sent and summed in bfloat16 or wider, within the bound.
No kernel may reach another device: no remote copies, remote signals or barrier semaphores. Data moves between devices by JAX's collectives and lax.ppermute only.
A program may use at most 128 MiB of HBM per device.

v0:
```python
import math
import jax
import jax.numpy as jnp
from jax import lax
from jax.sharding import PartitionSpec as P

NT = 2048
NF = 192
BIN0 = 16


def frequency_band_tables():
    sample_index = jnp.arange(NT, dtype=jnp.int32)
    bin_index = BIN0 + jnp.arange(NF, dtype=jnp.int32)
    phase = sample_index[:, None] * bin_index[None, :] % NT
    angle = phase.astype(jnp.float32) * (2.0 * math.pi / NT)
    cosine = jnp.cos(angle)
    sine = jnp.sin(angle)
    forward_table = jnp.stack([cosine, -sine], axis=2).reshape(NT, 2 * NF).astype(jnp.bfloat16)
    inverse_table = (
        (2.0 / NT * jnp.stack([cosine.T, -sine.T], axis=1)).reshape(2 * NF, NT).astype(jnp.bfloat16)
    )
    return (forward_table, inverse_table)


def forward_waves(kernel_real_part, kernel_imaginary, spectrum):
    spectral_real = spectrum[:, 0]
    spectral_imaginary = spectrum[:, 1]
    wave_real = jnp.einsum(
        "izb,ijb->ijz", kernel_real_part, spectral_real, preferred_element_type=jnp.float32
    ) - jnp.einsum(
        "izb,ijb->ijz", kernel_imaginary, spectral_imaginary, preferred_element_type=jnp.float32
    )
    wave_imag = jnp.einsum(
        "izb,ijb->ijz", kernel_real_part, spectral_imaginary, preferred_element_type=jnp.float32
    ) + jnp.einsum(
        "izb,ijb->ijz", kernel_imaginary, spectral_real, preferred_element_type=jnp.float32
    )
    return jnp.stack([wave_real, wave_imag], axis=1).astype(jnp.bfloat16)


def adjoint_terms(kernel_real_part, kernel_imaginary, spectrum):
    backward_real = spectrum[:, 0]
    backward_imaginary = spectrum[:, 1]
    term_real = jnp.einsum(
        "doy,dvo->vdy", kernel_real_part, backward_real, preferred_element_type=jnp.float32
    ) + jnp.einsum(
        "doy,dvo->vdy", kernel_imaginary, backward_imaginary, preferred_element_type=jnp.float32
    )
    term_imag = jnp.einsum(
        "doy,dvo->vdy", kernel_real_part, backward_imaginary, preferred_element_type=jnp.float32
    ) - jnp.einsum(
        "doy,dvo->vdy", kernel_imaginary, backward_real, preferred_element_type=jnp.float32
    )
    return jnp.stack([term_real, term_imag], axis=2)


def local(focusing, direct, kernel, onset_up, onset_back):
    forward_table, inverse_table = frequency_band_tables()
    kernel_real_part = kernel[0]
    kernel_imaginary = kernel[1]
    sample_index = jnp.arange(NT, dtype=jnp.int32)
    point_count = focusing.shape[0]
    recv_count = focusing.shape[1]
    bins_local = jnp.einsum(
        "tk,prt->kpr", forward_table, focusing, preferred_element_type=jnp.float32
    )
    bins_local = bins_local.astype(jnp.bfloat16).reshape(NF, 2, point_count, recv_count)
    everyone = lax.all_gather(bins_local, "src", axis=2, tiled=True)
    waves = forward_waves(
        kernel_real_part,
        kernel_imaginary,
        lax.all_to_all(everyone, "freq", split_axis=0, concat_axis=3, tiled=True),
    )
    timed = lax.all_to_all(waves, "freq", split_axis=2, concat_axis=0, tiled=True)
    up_points = timed.shape[2]
    source_count = timed.shape[3]
    signal = jnp.einsum(
        "kps,kt->pst",
        timed.reshape(2 * NF, up_points, source_count),
        inverse_table,
        preferred_element_type=jnp.float32,
    )
    upgoing = jnp.where(sample_index[None, None, :] < onset_up[:, :, None], signal, 0.0).astype(
        jnp.bfloat16
    )
    back_local = jnp.einsum(
        "tk,pst->kps", forward_table, upgoing, preferred_element_type=jnp.float32
    )
    back_local = back_local.astype(jnp.bfloat16).reshape(NF, 2, up_points, source_count)
    banded = lax.all_to_all(back_local, "freq", split_axis=0, concat_axis=2, tiled=True)
    partial_terms = adjoint_terms(kernel_real_part, kernel_imaginary, banded).astype(jnp.bfloat16)
    moved = lax.all_to_all(partial_terms, "freq", split_axis=3, concat_axis=1, tiled=True)
    summed = (
        lax.psum_scatter(moved, "src", scatter_dimension=0, tiled=True)
        .astype(jnp.float32)
        .astype(jnp.bfloat16)
    )
    back_count = summed.shape[3]
    trace = jnp.einsum(
        "pkr,kt->prt",
        summed.reshape(point_count, 2 * NF, back_count),
        inverse_table,
        preferred_element_type=jnp.float32,
    )
    cut = jnp.where(sample_index[None, None, :] < onset_back[:, :, None], trace, 0.0)
    updated = (direct.astype(jnp.float32) - cut).astype(jnp.bfloat16)
    return (upgoing, updated)


def solution(mesh):
    placed = (
        P("src", "freq", None),
        P("src", "freq", None),
        P(None, "freq", "src", None),
        P("freq", "src"),
        P("src", "freq"),
    )
    return jax.shard_map(
        local,
        mesh=mesh,
        in_specs=placed,
        out_specs=(P("freq", "src", None), P("src", "freq", None)),
        check_vma=False,
    )
```

profile of v0, /device:TPU:0, one launch (start us, length us, event | category | flops | bytes accessed | tf_op | source)
XLA Modules:
  0.0 504.8 jit_solution(12992001424295173069)
XLA Ops:
  7.2 0.0 copy-start
  7.2 0.0 all-gather.2.cloned.1.call-start
  7.2 6.9 %cosine_convert_fusion = (bf16[2048,192,1]{0,1,2:T(8,128)(2,1)S(1)}, bf16[2048,192,1]{0,1,2:T(8,128)(2,1)S(1)}) fusion(s32[192]{0:T(256)S(1)} %iota_add_fusion), kind=kLoop, calls=%fused_computation.57 | loop fusion | flops 6684672 | bytes 1573632 | tf_op jit(solution)/shard_map/convert.10
  14.2 0.1 pad_maximum_fusion.1
  14.3 2.8 copy.46
  17.1 3.6 convert_element_type.70
  20.7 2.7 fusion.58
  23.4 1.3 copy.48
  24.7 0.0 all-gather.2.cloned.1.call-update
  24.8 101.0 %all-gather.2.cloned.1.call-done = bf16[192,2,64,64]{3,2,1,0:T(8,128)(2,1)} async-done(((bf16[192,2,8,64]{3,2,1,0:T(8,128)(2,1)}), bf16[192,2,64,64]{3,2,1,0:T(8,128)(2,1)}) %all-gather.2.cloned.1.call-update) | async-done | bytes 3145744 | tf_op jit(solution)/shard_map/all_gather | solution.py:69
  125.8 12.7 %reshape.241 = bf16[16,2,49152]{2,1,0:T(2,128)(2,1)} reshape(bf16[192,2,64,64]{3,2,1,0:T(8,128)(2,1)} %all-gather.2.cloned.1.call-done) | data formatting | bytes 6291456
  138.5 4.9 all-to-all-start
  143.4 2.0 reshape.236
  145.4 37.0 %all-to-all-done = bf16[16,2,49152]{2,1,0:T(2,128)(2,1)} async-done(((bf16[16,2,49152]{2,1,0:T(2,128)(2,1)}), bf16[16,2,49152]{2,1,0:T(2,128)(2,1)}, u32[]{:S(2)}, u32[]{:S(2)}) %all-to-all-start) | async-done | bytes 3145760 | tf_op jit(solution)/shard_map/all_to_all | solution.py:73
  182.4 12.3 %reshape.242 = bf16[192,2,64,64]{3,2,1,0:T(8,128)(2,1)} reshape(bf16[16,2,49152]{2,1,0:T(2,128)(2,1)} %all-to-all-done) | data formatting | bytes 6291456
  194.7 11.1 %copy.49 = bf16[12,2,64,16,64]{4,3,2,0,1:T(8,128)(2,1)} copy(bf16[12,2,64,16,64]{4,2,1,0,3:T(8,128)(2,1)} %bitcast.132) | data formatting | bytes 6291456 | tf_op jit(solution)/shard_map/all_to_all | solution.py:73
  205.8 9.9 %all_to_all.53 = bf16[12,2,64,1024]{3,2,0,1:T(8,128)(2,1)} reshape(bf16[12,2,64,16,64]{4,3,2,0,1:T(8,128)(2,1)} %copy.49) | data formatting | bytes 6291456 | tf_op jit(solution)/shard_map/all_to_all | solution.py:73
  215.7 0.0 copy-start.4
  215.7 0.0 slice-start
  215.7 5.4 %fusion.4 = f32[12,64,256]{2,1,0:T(8,128)S(1)} fusion(bf16[2,12,256,1024]{3,2,1,0:T(8,128)(2,1)} %param.7, bf16[12,2,64,1024]{3,2,0,1:T(8,128)(2,1)} %all_to_all.53), kind=kOutput, calls=%fused_computation.6 | convolution fusion | flops 402653184 | bytes 8650752 | tf_op jit(solution)/shard_map/izb,ijb->ijz/dot_general | solution.py:36
  221.2 0.0 slice-start.1
  221.2 5.0 fusion.6
  226.2 0.0 slice-start.2
  226.2 5.0 fusion.70
  231.3 2.0 fusion.67
  233.3 0.1 pad_maximum_fusion.2
  233.4 1.7 copy.50
  235.1 8.9 %all-to-all-start.1 = ((bf16[12,2,64,256]{3,1,0,2:T(2,128)(2,1)}), bf16[12,2,64,256]{3,1,0,2:T(2,128)(2,1)S(1)}, u32[]{:S(2)}, u32[]{:S(2)}) async-start(bf16[12,2,64,256]{3,1,0,2:T(2,128)(2,1)} %copy.50), calls=%async_computation.1 | async-start | bytes 1572864 | tf_op jit(solution)/shard_map/all_to_all | solution.py:75
  244.0 0.2 reduce-scatter.2.cloned.1.call-start
  244.2 6.2 %fusion.74 = (f32[192,1,2048]{2,0,1:T(8,128)S(1)}, f32[192,1,2048]{2,0,1:T(8,128)S(1)}) fusion(s32[192]{0:T(256)S(1)} %iota_add_fusion), kind=kLoop, calls=%fused_computation.75 | loop fusion | flops 5898240 | bytes 3146496 | tf_op jit(solution)/shard_map/cos | solution.py:17
  250.4 0.2 fusion.26
  250.7 1.1 copy-done.3
  251.8 1.6 copy.52
  253.5 0.0 copy-start.6
  253.5 2.2 reshape.235
  255.7 1.9 all-to-all-done.1
  257.6 0.4 copy.51
  258.0 4.0 select_convert_fusion
  262.0 0.0 copy-start.8
  262.0 2.0 copy-done.8
  264.1 1.8 convolution_convert_fusion
  265.9 0.3 reshape.233
  266.2 0.5 copy.54
  266.7 16.9 %all_to_all.69 = bf16[192,2,4,256]{3,1,2,0:T(2,128)(2,1)S(1)} all-to-all(bf16[192,2,4,256]{3,1,2,0:T(2,128)(2,1)S(1)} %copy.54), channel_id=1, replica_groups=mesh['freq'=16,'src'=8] {'freq'}, dimensions={0} | all-to-all | bytes 1572864 | tf_op jit(solution)/shard_map/all_to_all | solution.py:91
  283.6 0.4 copy.65
  284.0 0.2 all_to_all.60
  284.2 0.0 slice-start.3
  284.2 4.1 fusion
  288.4 0.0 slice-start.4
  288.4 4.1 fusion.2
  292.5 0.0 slice-start.5
  292.5 4.2 fusion.49
  296.8 1.2 fusion.46
  298.0 2.0 pad_maximum_fusion
  300.0 15.9 %copy.56 = bf16[64,12,2,1024]{0,2,1,3:T(2,128)(2,1)} copy(bf16[64,12,2,1024]{3,0,1,2:T(8,128)(2,1)} %pad_maximum_fusion) | data formatting | bytes 6291456 | tf_op jit(solution)/shard_map/stack | solution.py:55
  315.9 12.7 %reshape.243 = bf16[16,2,49152]{2,1,0:T(2,128)(2,1)} reshape(bf16[1024,12,2,64]{3,2,1,0:T(2,128)(2,1)} %bitcast.133) | data formatting | bytes 6291456
  328.6 43.4 %all_to_all.70 = bf16[16,2,49152]{2,1,0:T(2,128)(2,1)} all-to-all(bf16[16,2,49152]{2,1,0:T(2,128)(2,1)} %reshape.243), channel_id=1, replica_groups=mesh['freq'=16,'src'=8] {'freq'}, dimensions={0} | all-to-all | bytes 6291456 | tf_op jit(solution)/shard_map/all_to_all | solution.py:93
  372.0 12.3 %reshape.244 = bf16[1024,12,2,64]{3,2,1,0:T(2,128)(2,1)} reshape(bf16[16,2,49152]{2,1,0:T(2,128)(2,1)} %all_to_all.70) | data formatting | bytes 6291456
  384.4 16.3 %copy.57 = bf16[64,12,2,16,64]{4,0,2,1,3:T(8,128)(2,1)} copy(bf16[64,12,2,16,64]{0,2,1,4,3:T(2,128)(2,1)} %bitcast.134) | data formatting | bytes 6291456 | tf_op jit(solution)/shard_map/all_to_all | solution.py:93
  400.7 9.1 %copy.58 = bf16[64,192,2,64]{1,3,2,0:T(8,128)(2,1)} copy(bf16[64,192,2,64]{3,0,2,1:T(8,128)(2,1)} %bitcast.135) | data formatting | bytes 6291456 | tf_op jit(solution)/shard_map/all_to_all | solution.py:93
  409.8 0.0 reduce-scatter.2.cloned.1.call-update
  409.8 0.0 copy-start.1
  409.8 82.9 %reduce-scatter.2.cloned.1.call-done = bf16[8,192,2,64]{1,3,2,0:T(8,128)(2,1)} async-done(((bf16[64,192,2,64]{1,3,2,0:T(8,128)(2,1)}), bf16[8,192,2,64]{1,3,2,0:T(8,128)(2,1)}) %reduce-scatter.2.cloned.1.call-update) | async-done | bytes 393232 | tf_op jit(solution)/shard_map/reduce_scatter | solution.py:95
  492.7 5.0 fusion.17
  (20 shorter events, 0.0 us)
Async XLA Ops:
  7.2 13.6 %copy-start = (bf16[8,64,2048]{2,1,0:T(8,128)(2,1)S(1)}, bf16[8,64,2048]{2,1,0:T(8,128)(2,1)}, u32[]{:S(2)}) copy-start(bf16[8,64,2048]{2,1,0:T(8,128)(2,1)} %param.5) | copy-start | bytes 6291460
  7.2 118.6 %all-gather.2.cloned.1.call-start = ((), (), s32[]{:S(2)}) async-start(), calls=%async_computation.5 | async-start | bytes 7077888 | tf_op jit(solution)/shard_map/all_gather | solution.py:69
  138.5 4.9 copy-start.2
  138.5 43.9 %all-to-all-start = ((bf16[16,2,49152]{2,1,0:T(2,128)(2,1)}), bf16[16,2,49152]{2,1,0:T(2,128)(2,1)}, u32[]{:S(2)}, u32[]{:S(2)}) async-start(bf16[16,2,49152]{2,1,0:T(2,128)(2,1)} %reshape.241), calls=%async_computation | async-start | bytes 6291456 | tf_op jit(solution)/shard_map/all_to_all | solution.py:73
  215.7 5.5 %copy-start.4 = (bf16[12,2,64,1024]{3,2,0,1:T(8,128)(2,1)S(1)}, bf16[12,2,64,1024]{3,2,0,1:T(8,128)(2,1)}, u32[]{:S(2)}) copy-start(bf16[12,2,64,1024]{3,2,0,1:T(8,128)(2,1)} %all_to_all.53) | copy-start | bytes 9437188
  215.7 15.5 %slice-start = ((s8[12582912]{0:T(1024)(128)(4,1)}), s8[4194304]{0:T(1024)(128)(4,1)S(1)}, s32[]{:S(2)}) async-start(s8[12582912]{0:T(1024)(128)(4,1)} %bitcast.128), calls=%async_computation.7 | async-start | bytes 8388608
  221.2 10.1 %slice-start.1 = ((s8[12582912]{0:T(1024)(128)(4,1)}), s8[4194304]{0:T(1024)(128)(4,1)S(1)}, s32[]{:S(2)}) async-start(s8[12582912]{0:T(1024)(128)(4,1)} %bitcast.128), calls=%async_computation.8 | async-start | bytes 8388608
  226.2 5.1 %slice-start.2 = ((s8[12582912]{0:T(1024)(128)(4,1)}), s8[4194304]{0:T(1024)(128)(4,1)S(1)}, s32[]{:S(2)}) async-start(s8[12582912]{0:T(1024)(128)(4,1)} %bitcast.128), calls=%async_computation.9 | async-start | bytes 8388608
  235.1 22.5 %all-to-all-start.1 = ((bf16[12,2,64,256]{3,1,0,2:T(2,128)(2,1)}), bf16[12,2,64,256]{3,1,0,2:T(2,128)(2,1)S(1)}, u32[]{:S(2)}, u32[]{:S(2)}) async-start(bf16[12,2,64,256]{3,1,0,2:T(2,128)(2,1)} %copy.50), calls=%async_computation.1 | async-start | bytes 1572864 | tf_op jit(solution)/shard_map/all_to_all | solution.py:75
  244.0 248.8 %reduce-scatter.2.cloned.1.call-start = ((), (), s32[]{:S(2)}) async-start(), calls=%async_computation.6 | async-start | bytes 4718592 | tf_op jit(solution)/shard_map/reduce_scatter | solution.py:95
  250.7 1.2 copy-start.3
  253.5 4.5 copy-start.6
  258.0 6.0 %copy-start.5 = (bf16[2048,384,1]{0,1,2:T(8,128)(2,1)S(1)}, bf16[2048,384,1]{0,1,2:T(8,128)(2,1)}, u32[]{:S(2)}) copy-start(bf16[2048,384,1]{0,1,2:T(8,128)(2,1)} %reshape.236) | copy-start | bytes 4718596
  262.0 2.0 copy-start.8
  284.2 12.6 %slice-start.3 = ((s8[12582912]{0:T(1024)(128)(4,1)}), s8[4194304]{0:T(1024)(128)(4,1)S(1)}, s32[]{:S(2)}) async-start(s8[12582912]{0:T(1024)(128)(4,1)} %bitcast.130), calls=%async_computation.10 | async-start | bytes 8388608
  288.4 8.4 %slice-start.4 = ((s8[12582912]{0:T(1024)(128)(4,1)}), s8[4194304]{0:T(1024)(128)(4,1)S(1)}, s32[]{:S(2)}) async-start(s8[12582912]{0:T(1024)(128)(4,1)} %bitcast.130), calls=%async_computation.11 | async-start | bytes 8388608
  292.5 4.3 slice-start.5
  409.8 82.9 %copy-start.7 = (s32[8,64]{1,0:T(8,128)S(1)}, s32[8,64]{1,0:T(8,128)}, u32[]{:S(2)}) copy-start(s32[8,64]{1,0:T(8,128)} %param.9) | copy-start | bytes 6148
  409.8 87.9 %copy-start.1 = (bf16[8,64,2048]{2,1,0:T(8,128)(2,1)S(1)}, bf16[8,64,2048]{2,1,0:T(8,128)(2,1)}, u32[]{:S(2)}) copy-start(bf16[8,64,2048]{2,1,0:T(8,128)(2,1)} %param.5) | copy-start | bytes 6291460
Sparse Core Ops, SparseCore 0:
  24.9 100.8 all-gather.1
  409.9 82.7 reduce-scatter.1
where the time goes:
time: 512 us; the launch traced here: 505 us
  waiting for transfers between devices  223 us (44%)
  local copies, waits for them, and re-layouts  133 us (26%)
  blocking collectives  60.3 us (12%)
  matrix products  44.7 us (9%)
  other arithmetic  15.6 us (3%)
  between operations  14.6 us (3%)
  starting transfers between devices  14.1 us (3%)
    all_gather x1, waiting for transfers between devices, local(): everyone = lax.all_gather(bins_local, 'src', axis=2, tiled=True)  101 us
    reduce_scatter x1, waiting for transfers between devices, local(): lax.psum_scatter(moved, 'src', scatter_dimension=0, tiled=True)  82.9 us
    unnamed x34, local copies, waits for them, and re-layouts  53.3 us
    all_to_all x1, blocking collectives, local(): lax.all_to_all(partial_terms, 'freq', split_axis=3, concat_axis=1, tiled=...  43.4 us
    all_to_all x1, waiting for transfers between devices, local(): lax.all_to_all(everyone, 'freq', split_axis=0, concat_axis=3, tiled=True)  37 us
    all_to_all x2, local copies, waits for them, and re-layouts, local(): lax.all_to_all(partial_terms, 'freq', split_axis=3, concat_axis=1, tiled=...  25.4 us
    all_to_all x2, local copies, waits for them, and re-layouts, local(): lax.all_to_all(everyone, 'freq', split_axis=0, concat_axis=3, tiled=True)  21 us
    all_to_all x1, blocking collectives, local(): lax.all_to_all(back_local, 'freq', split_axis=0, concat_axis=2, tiled=True)  16.9 us
  transfers between devices with their start and end apart: 4, of which 4 were waited for; matrix products, arithmetic and copies ran while one was open for 2% of the time, Pallas kernels for 0%

commit v1 on v0

--- a/solution.py
+++ b/solution.py
@@ -66,7 +66,8 @@
         "tk,prt->kpr", forward_table, focusing, preferred_element_type=jnp.float32
     )
     bins_local = bins_local.astype(jnp.bfloat16).reshape(NF, 2, point_count, recv_count)
-    everyone = lax.all_gather(bins_local, "src", axis=2, tiled=True)
+    sent = jnp.stack([bins_local] * lax.axis_size("src"))
+    everyone = jnp.concatenate(lax.all_to_all(sent, "src", 0, 0), axis=2)
     waves = forward_waves(
         kernel_real_part,
         kernel_imaginary,

time: 512 us -> 482 us (0.941)
  waiting for transfers between devices: 223 us -> 121 us
  blocking collectives: 60.3 us -> 119 us
  local copies, waits for them, and re-layouts: 133 us -> 144 us
    all_gather x1 -> x0, waiting for transfers between devices: 101 us -> none  [local(): everyone = lax.all_gather(bins_local, 'src', axis=2, tiled=True)]
    all_to_all x0 -> x1, blocking collectives: none -> 58.5 us  [local(): everyone = jnp.concatenate(lax.all_to_all(sent, 'src', 0, 0), axis=2)]
    reshape x0 -> x1, local copies, waits for them, and re-layouts: none -> 9.11 us  [local(): everyone = jnp.concatenate(lax.all_to_all(sent, 'src', 0, 0), axis=2)]
  transfers between devices with their start and end apart: 4 -> 3, of which waited for: 4 -> 3; matrix products, arithmetic and copies ran while one was open for 2% -> 3% of each run, Pallas kernels for 0% -> 0%
where the time goes in v1:
time: 482 us; the launch traced here: 473 us
  local copies, waits for them, and re-layouts  144 us (30%)
  waiting for transfers between devices  121 us (25%)
  blocking collectives  119 us (25%)
  matrix products  44.7 us (9%)
  other arithmetic  15.6 us (3%)
  between operations  14.6 us (3%)
  starting transfers between devices  14.4 us (3%)
    reduce_scatter x1, waiting for transfers between devices, local(): lax.psum_scatter(moved, 'src', scatter_dimension=0, tiled=True)  82 us
    all_to_all x1, blocking collectives, local(): everyone = jnp.concatenate(lax.all_to_all(sent, 'src', 0, 0), axis=2)  58.5 us
    unnamed x34, local copies, waits for them, and re-layouts  53.3 us
    all_to_all x1, blocking collectives, local(): lax.all_to_all(partial_terms, 'freq', split_axis=3, concat_axis=1, tiled=...  43.4 us
    all_to_all x1, waiting for transfers between devices, local(): lax.all_to_all(everyone, 'freq', split_axis=0, concat_axis=3, tiled=True)  37 us
    all_to_all x2, local copies, waits for them, and re-layouts, local(): lax.all_to_all(partial_terms, 'freq', split_axis=3, concat_axis=1, tiled=...  25.4 us
    all_to_all x2, local copies, waits for them, and re-layouts, local(): lax.all_to_all(everyone, 'freq', split_axis=0, concat_axis=3, tiled=True)  20.9 us
    all_to_all x1, blocking collectives, local(): lax.all_to_all(back_local, 'freq', split_axis=0, concat_axis=2, tiled=True)  16.9 us
  transfers between devices with their start and end apart: 3, of which 3 were waited for; matrix products, arithmetic and copies ran while one was open for 3% of the time, Pallas kernels for 0%

profile of v1, /device:TPU:0, one launch (start us, length us, event | category | flops | bytes accessed | tf_op | source)
XLA Modules:
  0.0 473.4 jit_solution(16305402035372880446)
XLA Ops:
  7.2 0.0 copy-start
  7.2 6.9 %cosine_convert_fusion = (bf16[2048,192,1]{0,1,2:T(8,128)(2,1)S(1)}, bf16[2048,192,1]{0,1,2:T(8,128)(2,1)S(1)}) fusion(s32[192]{0:T(256)S(1)} %iota_add_fusion), kind=kLoop, calls=%fused_computation.57 | loop fusion | flops 6684672 | bytes 1573632 | tf_op jit(solution)/shard_map/convert.10
  14.1 0.1 pad_maximum_fusion.1
  14.3 2.8 copy.54
  17.0 3.6 convert_element_type.70
  20.7 2.7 fusion.58
  23.4 0.5 copy.56
  23.9 0.7 copy.57
  24.5 0.5 stack.39
  25.1 58.5 %all_to_all.74 = bf16[8,192,2,8,64]{1,4,3,2,0:T(8,128)(2,1)S(1)} all-to-all(bf16[8,192,2,8,64]{1,4,3,2,0:T(8,128)(2,1)S(1)} %stack.39), channel_id=1, replica_groups=mesh['freq'=16,'src'=8] {'src'}, dimensions={0} | all-to-all | bytes 6291456 | tf_op jit(solution)/shard_map/all_to_all | solution.py:70
  83.5 2.3 copy.58
  85.8 9.1 %copy.59 = bf16[192,2,64,64]{3,2,1,0:T(8,128)(2,1)} copy(bf16[192,2,64,64]{0,3,2,1:T(8,128)(2,1)} %bitcast.139) | data formatting | bytes 6291456 | tf_op jit(solution)/shard_map/reshape | solution.py:70
  95.0 12.7 %reshape.247 = bf16[16,2,49152]{2,1,0:T(2,128)(2,1)} reshape(bf16[192,2,64,64]{3,2,1,0:T(8,128)(2,1)} %copy.59) | data formatting | bytes 6291456
  107.6 5.3 %all-to-all-start.1 = ((bf16[16,2,49152]{2,1,0:T(2,128)(2,1)}), bf16[16,2,49152]{2,1,0:T(2,128)(2,1)}, u32[]{:S(2)}, u32[]{:S(2)}) async-start(bf16[16,2,49152]{2,1,0:T(2,128)(2,1)} %reshape.247), calls=%async_computation.1 | async-start | bytes 6291456 | tf_op jit(solution)/shard_map/all_to_all | solution.py:74
  113.0 2.0 reshape.242
  115.0 37.0 %all-to-all-done.1 = bf16[16,2,49152]{2,1,0:T(2,128)(2,1)} async-done(((bf16[16,2,49152]{2,1,0:T(2,128)(2,1)}), bf16[16,2,49152]{2,1,0:T(2,128)(2,1)}, u32[]{:S(2)}, u32[]{:S(2)}) %all-to-all-start.1) | async-done | bytes 3145760 | tf_op jit(solution)/shard_map/all_to_all | solution.py:74
  152.0 12.3 %reshape.248 = bf16[192,2,64,64]{3,2,1,0:T(8,128)(2,1)} reshape(bf16[16,2,49152]{2,1,0:T(2,128)(2,1)} %all-to-all-done.1) | data formatting | bytes 6291456
  164.3 11.1 %copy.60 = bf16[12,2,64,16,64]{4,3,2,0,1:T(8,128)(2,1)} copy(bf16[12,2,64,16,64]{4,2,1,0,3:T(8,128)(2,1)} %bitcast.135) | data formatting | bytes 6291456 | tf_op jit(solution)/shard_map/all_to_all | solution.py:74
  175.3 9.9 %all_to_all.57 = bf16[12,2,64,1024]{3,2,0,1:T(8,128)(2,1)} reshape(bf16[12,2,64,16,64]{4,3,2,0,1:T(8,128)(2,1)} %copy.60) | data formatting | bytes 6291456 | tf_op jit(solution)/shard_map/all_to_all | solution.py:74
  185.2 0.0 copy-start.4
  185.2 0.0 slice-start
  185.3 5.4 %fusion.4 = f32[12,64,256]{2,1,0:T(8,128)S(1)} fusion(bf16[2,12,256,1024]{3,2,1,0:T(8,128)(2,1)} %param.7, bf16[12,2,64,1024]{3,2,0,1:T(8,128)(2,1)} %all_to_all.57), kind=kOutput, calls=%fused_computation.6 | convolution fusion | flops 402653184 | bytes 8650752 | tf_op jit(solution)/shard_map/izb,ijb->ijz/dot_general | solution.py:36
  190.7 0.0 slice-start.1
  190.7 5.0 %fusion.6 = f32[12,64,256]{2,1,0:T(8,128)S(1)} fusion(bf16[2,12,256,1024]{3,2,1,0:T(8,128)(2,1)} %param.7, bf16[12,2,64,1024]{3,2,0,1:T(8,128)(2,1)S(1)} %copy-done.4), kind=kOutput, calls=%fused_computation.8 | convolution fusion | flops 402653184 | bytes 8650752 | tf_op jit(solution)/shard_map/izb,ijb->ijz/dot_general | solution.py:31
  195.7 5.0 %fusion.70 = bf16[12,1,64,256]{3,2,0,1:T(8,128)(2,1)S(1)} fusion(f32[12,64,256]{2,1,0:T(8,128)S(1)} %fusion.4, bf16[2,12,256,1024]{3,2,1,0:T(8,128)(2,1)} %param.7, bf16[12,2,64,1024]{3,2,0,1:T(8,128)(2,1)S(1)} %copy-done.4), kind=kOutput, calls=%fused_computation.71 | convolution fusion | flops 403046400 | bytes 9043968 | tf_op jit(solution)/shard_map/izb,ijb->ijz/dot_general | solution.py:34
  200.8 2.0 fusion.67
  202.9 0.1 pad_maximum_fusion.2
  202.9 1.7 copy.61
  204.6 8.9 %all-to-all-start.2 = ((bf16[12,2,64,256]{3,1,0,2:T(2,128)(2,1)}), bf16[12,2,64,256]{3,1,0,2:T(2,128)(2,1)S(1)}, u32[]{:S(2)}, u32[]{:S(2)}) async-start(bf16[12,2,64,256]{3,1,0,2:T(2,128)(2,1)} %copy.61), calls=%async_computation.2 | async-start | bytes 1572864 | tf_op jit(solution)/shard_map/all_to_all | solution.py:76
  213.5 0.2 reduce-scatter.2.cloned.1.call-start
  213.7 6.2 %fusion.74 = (f32[192,1,2048]{2,0,1:T(8,128)S(1)}, f32[192,1,2048]{2,0,1:T(8,128)S(1)}) fusion(s32[192]{0:T(256)S(1)} %iota_add_fusion), kind=kLoop, calls=%fused_computation.75 | loop fusion | flops 5898240 | bytes 3146496 | tf_op jit(solution)/shard_map/cos | solution.py:17
  220.0 0.2 fusion.26
  220.2 1.2 copy-done.3
  221.4 1.6 copy.63
  223.0 0.0 copy-start.6
  223.0 2.2 reshape.241
  225.3 1.9 all-to-all-done.2
  227.2 0.4 copy.62
  227.6 4.0 select_convert_fusion
  231.6 0.0 copy-start.8
  231.6 2.0 copy-done.8
  233.6 1.8 convolution_convert_fusion
  235.4 0.3 reshape.239
  235.7 0.5 copy.65
  236.3 16.9 %all_to_all.75 = bf16[192,2,4,256]{3,1,2,0:T(2,128)(2,1)S(1)} all-to-all(bf16[192,2,4,256]{3,1,2,0:T(2,128)(2,1)S(1)} %copy.65), channel_id=1, replica_groups=mesh['freq'=16,'src'=8] {'freq'}, dimensions={0} | all-to-all | bytes 1572864 | tf_op jit(solution)/shard_map/all_to_all | solution.py:92
  253.2 0.4 copy.76
  253.6 0.2 all_to_all.64
  253.8 0.0 slice-start.3
  253.8 4.1 fusion
  257.9 0.0 slice-start.4
  258.0 4.1 fusion.2
  262.1 0.0 slice-start.5
  262.1 4.2 fusion.49
  266.4 1.2 fusion.46
  267.6 2.0 pad_maximum_fusion
  269.6 15.9 %copy.67 = bf16[64,12,2,1024]{0,2,1,3:T(2,128)(2,1)} copy(bf16[64,12,2,1024]{3,0,1,2:T(8,128)(2,1)} %pad_maximum_fusion) | data formatting | bytes 6291456 | tf_op jit(solution)/shard_map/stack | solution.py:55
  285.5 12.7 %reshape.249 = bf16[16,2,49152]{2,1,0:T(2,128)(2,1)} reshape(bf16[1024,12,2,64]{3,2,1,0:T(2,128)(2,1)} %bitcast.136) | data formatting | bytes 6291456
  298.2 43.4 %all_to_all.76 = bf16[16,2,49152]{2,1,0:T(2,128)(2,1)} all-to-all(bf16[16,2,49152]{2,1,0:T(2,128)(2,1)} %reshape.249), channel_id=1, replica_groups=mesh['freq'=16,'src'=8] {'freq'}, dimensions={0} | all-to-all | bytes 6291456 | tf_op jit(solution)/shard_map/all_to_all | solution.py:94
  341.6 12.3 %reshape.250 = bf16[1024,12,2,64]{3,2,1,0:T(2,128)(2,1)} reshape(bf16[16,2,49152]{2,1,0:T(2,128)(2,1)} %all_to_all.76) | data formatting | bytes 6291456
  353.9 16.3 %copy.68 = bf16[64,12,2,16,64]{4,0,2,1,3:T(8,128)(2,1)} copy(bf16[64,12,2,16,64]{0,2,1,4,3:T(2,128)(2,1)} %bitcast.137) | data formatting | bytes 6291456 | tf_op jit(solution)/shard_map/all_to_all | solution.py:94
  370.1 9.1 %copy.69 = bf16[64,192,2,64]{1,3,2,0:T(8,128)(2,1)} copy(bf16[64,192,2,64]{3,0,2,1:T(8,128)(2,1)} %bitcast.138) | data formatting | bytes 6291456 | tf_op jit(solution)/shard_map/all_to_all | solution.py:94
  379.2 0.0 reduce-scatter.2.cloned.1.call-update
  379.3 82.0 %reduce-scatter.2.cloned.1.call-done = bf16[8,192,2,64]{1,3,2,0:T(8,128)(2,1)} async-done(((bf16[64,192,2,64]{1,3,2,0:T(8,128)(2,1)}), bf16[8,192,2,64]{1,3,2,0:T(8,128)(2,1)}) %reduce-scatter.2.cloned.1.call-update) | async-done | bytes 393232 | tf_op jit(solution)/shard_map/reduce_scatter | solution.py:96
  461.3 5.0 %fusion.17 = bf16[8,64,2048]{2,1,0:T(8,128)(2,1)} fusion(bf16[8,64,2048]{2,1,0:T(8,128)(2,1)} %param.6, bf16[8,192,2,64]{1,3,2,0:T(8,128)(2,1)} %reduce-scatter.2.cloned.1.call-done, s32[8,64]{1,0:T(8,128)S(1)} %copy-done.7, bf16[192,2,2048]{2,0,1:T(8,128)(2,1)} %copy-done.3), kind=kOutput, calls=%fused_computation.20 | convolution fusion | flops 810549248 | bytes 6162432 | tf_op jit(solution)/shard_map/pkr,kt->prt/dot_general | solution.py:101
  (22 shorter events, 0.0 us)
Async XLA Ops:
  7.2 13.5 %copy-start = (bf16[8,64,2048]{2,1,0:T(8,128)(2,1)S(1)}, bf16[8,64,2048]{2,1,0:T(8,128)(2,1)}, u32[]{:S(2)}) copy-start(bf16[8,64,2048]{2,1,0:T(8,128)(2,1)} %param.5) | copy-start | bytes 6291460
  107.6 5.4 %copy-start.2 = (bf16[2048,192,2]{0,2,1:T(2,128)(2,1)S(1)}, bf16[2048,192,2]{0,2,1:T(2,128)(2,1)}, u32[]{:S(2)}) copy-start(bf16[2048,192,2]{0,2,1:T(2,128)(2,1)} %copy.54) | copy-start | bytes 4718596
  107.6 44.3 %all-to-all-start.1 = ((bf16[16,2,49152]{2,1,0:T(2,128)(2,1)}), bf16[16,2,49152]{2,1,0:T(2,128)(2,1)}, u32[]{:S(2)}, u32[]{:S(2)}) async-start(bf16[16,2,49152]{2,1,0:T(2,128)(2,1)} %reshape.247), calls=%async_computation.1 | async-start | bytes 6291456 | tf_op jit(solution)/shard_map/all_to_all | solution.py:74
  185.2 5.5 %copy-start.4 = (bf16[12,2,64,1024]{3,2,0,1:T(8,128)(2,1)S(1)}, bf16[12,2,64,1024]{3,2,0,1:T(8,128)(2,1)}, u32[]{:S(2)}) copy-start(bf16[12,2,64,1024]{3,2,0,1:T(8,128)(2,1)} %all_to_all.57) | copy-start | bytes 9437188
  185.2 15.5 %slice-start = ((s8[12582912]{0:T(1024)(128)(4,1)}), s8[4194304]{0:T(1024)(128)(4,1)S(1)}, s32[]{:S(2)}) async-start(s8[12582912]{0:T(1024)(128)(4,1)} %bitcast.131), calls=%async_computation.7 | async-start | bytes 8388608
  190.7 10.1 %slice-start.1 = ((s8[12582912]{0:T(1024)(128)(4,1)}), s8[4194304]{0:T(1024)(128)(4,1)S(1)}, s32[]{:S(2)}) async-start(s8[12582912]{0:T(1024)(128)(4,1)} %bitcast.131), calls=%async_computation.8 | async-start | bytes 8388608
  195.7 5.1 %slice-start.2 = ((s8[12582912]{0:T(1024)(128)(4,1)}), s8[4194304]{0:T(1024)(128)(4,1)S(1)}, s32[]{:S(2)}) async-start(s8[12582912]{0:T(1024)(128)(4,1)} %bitcast.131), calls=%async_computation.9 | async-start | bytes 8388608
  204.6 22.5 %all-to-all-start.2 = ((bf16[12,2,64,256]{3,1,0,2:T(2,128)(2,1)}), bf16[12,2,64,256]{3,1,0,2:T(2,128)(2,1)S(1)}, u32[]{:S(2)}, u32[]{:S(2)}) async-start(bf16[12,2,64,256]{3,1,0,2:T(2,128)(2,1)} %copy.61), calls=%async_computation.2 | async-start | bytes 1572864 | tf_op jit(solution)/shard_map/all_to_all | solution.py:76
  213.5 247.8 %reduce-scatter.2.cloned.1.call-start = ((), (), s32[]{:S(2)}) async-start(), calls=%async_computation.6 | async-start | bytes 4718592 | tf_op jit(solution)/shard_map/reduce_scatter | solution.py:96
  220.2 1.2 copy-start.3
  223.0 4.5 copy-start.6
  227.6 6.0 %copy-start.5 = (bf16[2048,384,1]{0,1,2:T(8,128)(2,1)S(1)}, bf16[2048,384,1]{0,1,2:T(8,128)(2,1)}, u32[]{:S(2)}) copy-start(bf16[2048,384,1]{0,1,2:T(8,128)(2,1)} %reshape.242) | copy-start | bytes 4718596
  231.6 2.0 copy-start.8
  253.8 12.6 %slice-start.3 = ((s8[12582912]{0:T(1024)(128)(4,1)}), s8[4194304]{0:T(1024)(128)(4,1)S(1)}, s32[]{:S(2)}) async-start(s8[12582912]{0:T(1024)(128)(4,1)} %bitcast.133), calls=%async_computation.10 | async-start | bytes 8388608
  257.9 8.4 %slice-start.4 = ((s8[12582912]{0:T(1024)(128)(4,1)}), s8[4194304]{0:T(1024)(128)(4,1)S(1)}, s32[]{:S(2)}) async-start(s8[12582912]{0:T(1024)(128)(4,1)} %bitcast.133), calls=%async_computation.11 | async-start | bytes 8388608
  262.1 4.3 slice-start.5
  379.2 82.1 %copy-start.7 = (s32[8,64]{1,0:T(8,128)S(1)}, s32[8,64]{1,0:T(8,128)}, u32[]{:S(2)}) copy-start(s32[8,64]{1,0:T(8,128)} %param.9) | copy-start | bytes 6148
  379.3 87.1 %copy-start.1 = (bf16[8,64,2048]{2,1,0:T(8,128)(2,1)S(1)}, bf16[8,64,2048]{2,1,0:T(8,128)(2,1)}, u32[]{:S(2)}) copy-start(bf16[8,64,2048]{2,1,0:T(8,128)(2,1)} %param.5) | copy-start | bytes 6291460
Sparse Core Ops, SparseCore 0:
  379.4 81.8 reduce-scatter.1
